TPU v7x, 256 devices: a whole 4x4x8 slice. The times are simulated.
256 devices in a mesh: row: 16 (over z, y_lo), col: 16 (over y_hi, x, core).
Axes of the slice: x: 4, y: 4 (y_hi: 2, y_lo: 2; y = y_hi * 2 + y_lo), z: 8, core: 2. Of those that a mesh axis runs over, the one named last changes fastest.
Arguments:
- ancestor: float32 [8192, 8192], P('row', 'col'), may hold values from -0.0625 to 0.0625
- factor: float32 [8192, 16, 128], P(('row', 'col')), may hold values from -1.5 to 1.5
- diag_inv: float32 [16, 128, 128], replicated, may hold values from -6 to 6
- structure: int32 [16, 768], replicated, may hold values from 0 to 1023, as said below
Outputs:
- inverse_panel: float32 [8192, 16, 128], P(('row', 'col'))
- inverse_diagonal: float32 [16, 128, 128], replicated
Inputs may be any that keep to these rules, and one draw needn't show every extreme that they name: Each row of structure lists 768 different block numbers, in no particular order.
All inputs are finite; a program needn't handle non-finite values.
Results may differ from a plain program's by a relative error of at most 0.00007.
Values sent between devices are 32-bit elements; how exact they have to be, the bound alone decides.
No kernel may reach another device: no remote copies, remote signals or barrier semaphores. Data moves between devices by JAX's collectives and lax.ppermute only.
A program may use at most 64 MiB of HBM per device.

v0:
```python
import jax
import jax.numpy as jnp
from jax import lax
from jax.sharding import PartitionSpec as P

RB = 8


def spread_2(value, axis, source):
    kept = jnp.where(lax.axis_index(axis) == source, value, 0).astype(value.dtype)
    return lax.psum(kept, axis)


def per_device(ancestor, factor, diag_inv, structure):
    row_devices = lax.axis_size("row")
    col_devices = lax.axis_size("col")
    ratio = row_devices // col_devices
    local_rows = factor.shape[0]
    width = factor.shape[2]
    first_row = (lax.axis_index("row") * col_devices + lax.axis_index("col")) * local_rows
    block_ids = (first_row + jnp.arange(local_rows, dtype=jnp.int32)) // RB
    matches = block_ids[:, None, None] == structure[None, :, :]
    row_mask = jnp.any(matches, axis=2).astype(jnp.float32)
    masked = factor * row_mask[:, :, None]
    count_sib = masked.shape[1]
    spread = masked.reshape(local_rows, count_sib * width)
    block_row = lax.all_gather(spread, "col", axis=0, tiled=True)
    received = spread_2(block_row, "row", lax.axis_index("col") * ratio + 0)
    summed = lax.psum_scatter(
        jnp.dot(
            ancestor, received, precision=lax.Precision.HIGHEST, preferred_element_type=jnp.float32
        ),
        "col",
        scatter_dimension=0,
        tiled=True,
    )
    panel = -summed.reshape(local_rows, count_sib, width)
    panel = panel * row_mask[:, :, None]
    local_update = jnp.einsum("bsw,bsv->swv", masked, panel, precision=lax.Precision.HIGHEST)
    total_update = lax.psum(local_update, ("row", "col"))
    return (panel, diag_inv - total_update)


def solution(mesh):
    placed = (P("row", "col"), P(("row", "col"), None, None), P(), P())
    return jax.shard_map(
        per_device,
        mesh=mesh,
        in_specs=placed,
        out_specs=(P(("row", "col"), None, None), P()),
        check_vma=False,
    )
```

profile of v0, /device:TPU:2, one launch (start us, length us, event | category | flops | bytes accessed | tf_op | source)
XLA Modules:
  0.0 657.8 jit_solution(703054387542532473)
XLA Ops:
  7.2 0.0 copy-start
  7.2 0.0 all-gather.2.cloned.1.call-start
  7.2 1.6 compare_reduce_fusion
  8.8 1.1 broadcast_multiply_fusion.1
  9.9 0.8 copy.23
  10.7 0.0 all-gather.2.cloned.1.call-update
  10.7 0.0 all-reduce.3.cloned.1.call-start
  10.8 64.4 %all-gather.2.cloned.1.call-done = f32[512,2048]{1,0:T(8,128)} async-done(((f32[32,2048]{1,0:T(8,128)}), f32[512,2048]{1,0:T(8,128)}) %all-gather.2.cloned.1.call-update) | async-done | bytes 4194320 | tf_op jit(solution)/shard_map/all_gather | solution.py:27
  75.2 2.5 broadcast_select_fusion
  77.7 0.0 all-reduce.3.cloned.1.call-update
  77.7 0.0 reduce-scatter.4.cloned.1.call-start
  77.8 199.0 %all-reduce.3.cloned.1.call-done = f32[512,2048]{1,0:T(8,128)} async-done(((f32[512,2048]{1,0:T(8,128)}), f32[512,2048]{1,0:T(8,128)}) %all-reduce.3.cloned.1.call-update) | async-done | bytes 4194320 | tf_op jit(solution)/shard_map/psum | solution.py:11
  276.8 0.0 copy-done
  276.8 16.3 %convolution_bitcast_fusion = f32[512,2048]{0,1:T(8,128)} fusion(f32[512,2048]{1,0:T(8,128)} %all-reduce.3.cloned.1.call-done, f32[512,512]{1,0:T(8,128)S(1)} %copy-done), kind=kOutput, calls=%fused_computation | convolution fusion | flops 6442450944 | bytes 9437184 | tf_op jit(solution)/shard_map/dot_general | solution.py:30
  293.0 5.4 copy.15
  298.4 0.0 reduce-scatter.4.cloned.1.call-update
  298.5 0.0 all-reduce.5.cloned.1.call-start
  298.5 88.3 %reduce-scatter.4.cloned.1.call-done = f32[32,2048]{1,0:T(8,128)} async-done(((f32[512,2048]{1,0:T(8,128)}), f32[32,2048]{1,0:T(8,128)}) %reduce-scatter.4.cloned.1.call-update) | async-done | bytes 262160
  386.8 1.3 copy.16
  388.1 0.1 neg.6
  388.2 0.3 copy.12
  388.5 0.1 broadcast_multiply_fusion
  388.7 0.0 copy-start.1
  388.7 2.8 fusion
  391.5 0.0 all-reduce.5.cloned.1.call-update
  391.5 257.1 %all-reduce.5.cloned.1.call-done = f32[16,128,128]{2,1,0:T(8,128)} async-done(((f32[16,128,128]{2,1,0:T(8,128)}), f32[16,128,128]{2,1,0:T(8,128)}) %all-reduce.5.cloned.1.call-update) | async-done | bytes 1048592 | tf_op jit(solution)/shard_map/psum | solution.py:40
  648.6 2.6 sub.10
  651.3 0.0 copy-done.1
  (2 shorter events, 0.0 us)
Async XLA Ops:
  7.2 269.6 %copy-start = (f32[512,512]{1,0:T(8,128)S(1)}, f32[512,512]{1,0:T(8,128)}, u32[]{:S(2)}) copy-start(f32[512,512]{1,0:T(8,128)} %param.4) | copy-start | bytes 3145732
  7.2 68.0 %all-gather.2.cloned.1.call-start = ((), (), s32[]{:S(2)}) async-start(), calls=%async_computation.1 | async-start | bytes 4456448 | tf_op jit(solution)/shard_map/all_gather | solution.py:27
  10.7 266.0 %all-reduce.3.cloned.1.call-start = ((), (), s32[]{:S(2)}) async-start(), calls=%async_computation.2 | async-start | bytes 8388608 | tf_op jit(solution)/shard_map/psum | solution.py:11
  77.7 309.1 %reduce-scatter.4.cloned.1.call-start = ((), (), s32[]{:S(2)}) async-start(), calls=%async_computation.4 | async-start | bytes 4456448
  298.5 350.2 %all-reduce.5.cloned.1.call-start = ((), (), s32[]{:S(2)}) async-start(), calls=%async_computation.3 | async-start | bytes 2097152 | tf_op jit(solution)/shard_map/psum | solution.py:40
  388.7 262.6 %copy-start.1 = (f32[32,16,128]{2,1,0:T(8,128)}, f32[32,16,128]{2,1,0:T(8,128)S(1)}, u32[]{:S(2)}) copy-start(f32[32,16,128]{2,1,0:T(8,128)S(1)} %broadcast_multiply_fusion) | copy-start | bytes 786436
Sparse Core Ops, SparseCore 0:
  11.3 63.8 all-gather.1
  77.8 198.8 all-reduce.2
  298.6 88.2 reduce-scatter.3
  393.6 254.9 all-reduce.4
where the time goes:
time: 658 us
  waiting for transfers between devices  609 us (93%)
  matrix products  19.1 us (3%)
  between operations  13.8 us (2%)
  other arithmetic  8.03 us (1%)
  local copies, waits for them, and re-layouts  7.8 us (1%)
    psum x1, waiting for transfers between devices, per_device(): total_update = lax.psum(local_update, ('row', 'col'))  257 us
    psum x1, waiting for transfers between devices, spread_2(): return lax.psum(kept, axis)  199 us
    unnamed x5, waiting for transfers between devices  88.4 us
    all_gather x1, waiting for transfers between devices, per_device(): block_row = lax.all_gather(spread, 'col', axis=0, tiled=True)  64.4 us
    dot_general x1, matrix products, per_device(): jnp.dot(ancestor, received, precision=lax.Precision.HIGHEST, preferred_el...  16.3 us
  transfers between devices with their start and end apart: 4, of which 4 were waited for; matrix products, arithmetic and copies ran while one was open for 0% of the time, Pallas kernels for 0%

commit v1 on v0

--- a/solution.py
+++ b/solution.py
@@ -37,7 +37,7 @@
     panel = -summed.reshape(local_rows, count_sib, width)
     panel = panel * row_mask[:, :, None]
     local_update = jnp.einsum("bsw,bsv->swv", masked, panel, precision=lax.Precision.HIGHEST)
-    total_update = lax.psum(local_update, ("row", "col"))
+    total_update = lax.psum(lax.psum(local_update, "row"), "col")
     return (panel, diag_inv - total_update)
 
 

time: 658 us -> 688 us (1.046)
  waiting for transfers between devices: 609 us -> 634 us
    psum x1 -> x2, waiting for transfers between devices: 257 us -> 282 us  [per_device(): total_update = lax.psum(lax.psum(local_update, 'row'), 'col')]
    unnamed x5 -> x6, waiting for transfers between devices: 88.4 us -> 88.4 us
  transfers between devices with their start and end apart: 4 -> 5, of which waited for: 4 -> 5; matrix products, arithmetic and copies ran while one was open for 0% -> 0% of each run, Pallas kernels for 0% -> 0%
where the time goes in v1:
time: 688 us; the launch traced here: 683 us
  waiting for transfers between devices  634 us (92%)
  matrix products  19.1 us (3%)
  between operations  13.9 us (2%)
  other arithmetic  8.03 us (1%)
  local copies, waits for them, and re-layouts  7.8 us (1%)
    psum x2, waiting for transfers between devices, per_device(): total_update = lax.psum(lax.psum(local_update, 'row'), 'col')  282 us
    psum x1, waiting for transfers between devices, spread_2(): return lax.psum(kept, axis)  199 us
    unnamed x6, waiting for transfers between devices  88.4 us
    all_gather x1, waiting for transfers between devices, per_device(): block_row = lax.all_gather(spread, 'col', axis=0, tiled=True)  64.4 us
    dot_general x1, matrix products, per_device(): jnp.dot(ancestor, received, precision=lax.Precision.HIGHEST, preferred_el...  16.3 us
  transfers between devices with their start and end apart: 5, of which 5 were waited for; matrix products, arithmetic and copies ran while one was open for 0% of the time, Pallas kernels for 0%

profile of v1, /device:TPU:2, one launch (start us, length us, event | category | flops | bytes accessed | tf_op | source)
XLA Modules:
  0.0 682.5 jit_solution(16789772689252889416)
XLA Ops:
  7.2 0.0 copy-start
  7.2 0.0 all-gather.2.cloned.1.call-start
  7.2 1.6 compare_reduce_fusion
  8.8 1.1 broadcast_multiply_fusion.1
  9.9 0.8 copy.23
  10.7 0.0 all-gather.2.cloned.1.call-update
  10.7 0.0 all-reduce.4.cloned.1.call-start
  10.8 64.4 %all-gather.2.cloned.1.call-done = f32[512,2048]{1,0:T(8,128)} async-done(((f32[32,2048]{1,0:T(8,128)}), f32[512,2048]{1,0:T(8,128)}) %all-gather.2.cloned.1.call-update) | async-done | bytes 4194320 | tf_op jit(solution)/shard_map/all_gather | solution.py:27
  75.2 2.5 broadcast_select_fusion
  77.7 0.0 all-reduce.4.cloned.1.call-update
  77.7 0.0 reduce-scatter.4.cloned.1.call-start
  77.8 199.0 %all-reduce.4.cloned.1.call-done = f32[512,2048]{1,0:T(8,128)} async-done(((f32[512,2048]{1,0:T(8,128)}), f32[512,2048]{1,0:T(8,128)}) %all-reduce.4.cloned.1.call-update) | async-done | bytes 4194320 | tf_op jit(solution)/shard_map/psum | solution.py:11
  276.8 0.0 copy-done
  276.8 16.3 %convolution_bitcast_fusion = f32[512,2048]{0,1:T(8,128)} fusion(f32[512,2048]{1,0:T(8,128)} %all-reduce.4.cloned.1.call-done, f32[512,512]{1,0:T(8,128)S(1)} %copy-done), kind=kOutput, calls=%fused_computation | convolution fusion | flops 6442450944 | bytes 9437184 | tf_op jit(solution)/shard_map/dot_general | solution.py:30
  293.0 5.4 copy.15
  298.4 0.0 reduce-scatter.4.cloned.1.call-update
  298.5 0.0 all-reduce.6.cloned.1.call-start
  298.5 88.3 %reduce-scatter.4.cloned.1.call-done = f32[32,2048]{1,0:T(8,128)} async-done(((f32[512,2048]{1,0:T(8,128)}), f32[32,2048]{1,0:T(8,128)}) %reduce-scatter.4.cloned.1.call-update) | async-done | bytes 262160
  386.8 1.3 copy.16
  388.1 0.1 neg.6
  388.2 0.3 copy.12
  388.5 0.1 broadcast_multiply_fusion
  388.7 0.0 copy-start.1
  388.7 2.8 fusion
  391.5 0.0 all-reduce.6.cloned.1.call-update
  391.5 0.0 all-reduce.8.cloned.1.call-start
  391.6 138.6 %all-reduce.6.cloned.1.call-done = f32[16,128,128]{2,1,0:T(8,128)} async-done(((f32[16,128,128]{2,1,0:T(8,128)}), f32[16,128,128]{2,1,0:T(8,128)}) %all-reduce.6.cloned.1.call-update) | async-done | bytes 1048592 | tf_op jit(solution)/shard_map/psum | solution.py:40
  530.1 0.0 all-reduce.8.cloned.1.call-update
  530.1 143.2 %all-reduce.8.cloned.1.call-done = f32[16,128,128]{2,1,0:T(8,128)} async-done(((f32[16,128,128]{2,1,0:T(8,128)}), f32[16,128,128]{2,1,0:T(8,128)}) %all-reduce.8.cloned.1.call-update) | async-done | bytes 1048592 | tf_op jit(solution)/shard_map/psum | solution.py:40
  673.3 2.6 sub.10
  676.0 0.0 copy-done.1
  (2 shorter events, 0.0 us)
Async XLA Ops:
  7.2 269.6 %copy-start = (f32[512,512]{1,0:T(8,128)S(1)}, f32[512,512]{1,0:T(8,128)}, u32[]{:S(2)}) copy-start(f32[512,512]{1,0:T(8,128)} %param.4) | copy-start | bytes 3145732
  7.2 68.0 %all-gather.2.cloned.1.call-start = ((), (), s32[]{:S(2)}) async-start(), calls=%async_computation.1 | async-start | bytes 4456448 | tf_op jit(solution)/shard_map/all_gather | solution.py:27
  10.7 266.0 %all-reduce.4.cloned.1.call-start = ((), (), s32[]{:S(2)}) async-start(), calls=%async_computation.2 | async-start | bytes 8388608 | tf_op jit(solution)/shard_map/psum | solution.py:11
  77.7 309.1 %reduce-scatter.4.cloned.1.call-start = ((), (), s32[]{:S(2)}) async-start(), calls=%async_computation.5 | async-start | bytes 4456448
  298.5 231.7 %all-reduce.6.cloned.1.call-start = ((), (), s32[]{:S(2)}) async-start(), calls=%async_computation.3 | async-start | bytes 2097152 | tf_op jit(solution)/shard_map/psum | solution.py:40
  388.7 287.3 %copy-start.1 = (f32[32,16,128]{2,1,0:T(8,128)}, f32[32,16,128]{2,1,0:T(8,128)S(1)}, u32[]{:S(2)}) copy-start(f32[32,16,128]{2,1,0:T(8,128)S(1)} %broadcast_multiply_fusion) | copy-start | bytes 786436
  391.5 281.8 %all-reduce.8.cloned.1.call-start = ((), (), s32[]{:S(2)}) async-start(), calls=%async_computation.4 | async-start | bytes 2097152 | tf_op jit(solution)/shard_map/psum | solution.py:40
Sparse Core Ops, SparseCore 0:
  11.3 63.8 all-gather.1
  77.8 198.8 all-reduce.3
  298.6 88.2 reduce-scatter.3
  391.6 138.4 all-reduce.5
  532.6 140.6 all-reduce.7
